TPU v7x, 32 devices: a whole 2x2x4 slice. The times are simulated.
32 devices in a mesh: gx: 4 (over x, core), gy: 8 (over z, y).
Axes of the slice: x: 2, y: 2, z: 4, core: 2. Of those that a mesh axis runs over, the one named last changes fastest.
Arguments:
- field: float32 [12, 64, 64, 128], P(None, 'gx', 'gy'), may hold values from -16 to 16
- diffusion: float32 [12], replicated, may hold values from 0.02 to 0.15
- prefactor: float32 [12], replicated, may hold values from 0.05 to 0.3
- activation: float32 [12], replicated, may hold values from 0.5 to 2
- mixing: float32 [12, 12], replicated, may hold values from -1.75 to 1.75
- basis_x: float32 [64, 64], P('gx'), may hold values from -1 to 1, as said below
- basis_y: float32 [64, 64], P('gy'), may hold values from -1 to 1, as said below
- basis_z: float32 [128, 32], replicated, may hold values from -1 to 1, as said below
- basis_v: float32 [12, 6], replicated, may hold values from -1 to 1, as said below
Outputs:
- state: float32 [12, 64, 64, 128], P(None, 'gx', 'gy')
- recon: float32 [12, 64, 64, 128], P(None, 'gx', 'gy')
- residual: float32 [12], replicated
Inputs may be any that keep to these rules, and one draw needn't show every extreme that they name: `basis_x`: its 64 columns are mutually orthogonal, each of norm between 0.5 and 1. `basis_y`: its 64 columns are orthonormal. `basis_z`: its 32 columns are orthonormal. `basis_v`: its 6 columns are orthonormal.
All inputs are finite; a program needn't handle non-finite values.
Results may differ from a plain program's by a relative error of at most 0.00013.
Values sent between devices are 32-bit elements; how exact they have to be, the bound alone decides.
No kernel may reach another device: no remote copies, remote signals or barrier semaphores. Data moves between devices by JAX's collectives and lax.ppermute only.
A program may use at most 64 MiB of HBM per device.

v0:
```python
import jax
import jax.numpy as jnp
from jax import lax
from jax.sharding import PartitionSpec as P

HIGH = lax.Precision.HIGHEST


def padded_2(array, sides, width):
    for axis, dim in sides:
        peers, length = (lax.axis_size(axis), array.shape[dim])
        up = [(i, (i + 1) % peers) for i in range(peers - 1)]
        down = [(j, i) for i, j in up]
        last = lax.slice_in_dim(array, length - width, length, axis=dim)
        first = lax.slice_in_dim(array, 0, width, axis=dim)
        before = lax.ppermute(last, axis, up)
        after = lax.ppermute(first, axis, down)
        array = jnp.concatenate([before, array, after], axis=dim)
    return array


def lap_core(padded):
    centre = padded[:, 1:-1, 1:-1, 1:-1]
    summed = padded[:, 2:, 1:-1, 1:-1] + padded[:, :-2, 1:-1, 1:-1]
    summed = summed + padded[:, 1:-1, 2:, 1:-1] + padded[:, 1:-1, :-2, 1:-1]
    summed = summed + padded[:, 1:-1, 1:-1, 2:] + padded[:, 1:-1, 1:-1, :-2]
    return summed - 6.0 * centre


def reaction(centre, coeffs):
    diffusion, prefactor, activation, mixing = coeffs
    temper = 1.5 + jnp.tanh(centre[0])
    rate_terms = (
        prefactor[:, None, None, None]
        * jnp.exp(-activation[:, None, None, None] / temper[None])
        * centre
    )
    return jnp.einsum("vw,wxyz->vxyz", mixing, rate_terms, precision=HIGH)


def tendency(rimmed, centre, coeffs):
    padded = jnp.pad(rimmed, ((0, 0), (0, 0), (0, 0), (1, 1)))
    return coeffs[0][:, None, None, None] * lap_core(padded) + reaction(centre, coeffs)


def inside_mask(rows_x, rows_y):
    pos_x = lax.axis_index("gx") * rows_x + jnp.arange(rows_x + 2) - 1
    pos_y = lax.axis_index("gy") * rows_y + jnp.arange(rows_y + 2) - 1
    in_x = (pos_x >= 0) & (pos_x < rows_x * lax.axis_size("gx"))
    in_y = (pos_y >= 0) & (pos_y < rows_y * lax.axis_size("gy"))
    return in_x[:, None] & in_y[None, :]


def step_deep(state, coeffs, inside):
    wide = padded_2(state, (("gx", 1), ("gy", 2)), 2)
    centre = wide[:, 1:-1, 1:-1]
    section_wide = centre + tendency(wide, centre, coeffs)
    section_wide = jnp.where(inside[None, :, :, None], section_wide, 0.0)
    section = section_wide[:, 1:-1, 1:-1]
    return 0.5 * (state + section + tendency(section_wide, section, coeffs))


def on_device(field, diffusion, prefactor, activation, mixing, basis_x, basis_y, basis_z, basis_v):
    coeffs = (diffusion, prefactor, activation, mixing)
    rows_x = field.shape[1]
    rows_y = field.shape[2]
    state = field
    inside = inside_mask(rows_x, rows_y)
    state = step_deep(state, coeffs, inside)
    rank_z = basis_z.shape[1]
    rank_v = basis_v.shape[1]
    width = rank_z * rank_v
    proj_z = jnp.einsum("vxyz,zr->vxyr", state, basis_z, precision=HIGH)
    packed = jnp.einsum("vxyr,vs->xyrs", proj_z, basis_v, precision=HIGH)
    packed = packed.reshape(rows_x, rows_y, width)
    columns = basis_x
    part_x = lax.psum_scatter(
        jnp.einsum("xa,xyk->ayk", columns, packed, precision=HIGH),
        "gx",
        scatter_dimension=0,
        tiled=True,
    )
    core_block = jnp.einsum("ayk,yb->abk", part_x, basis_y, precision=HIGH)
    core_block = lax.psum(core_block, "gy")
    mixed_y = jnp.einsum("abk,yb->ayk", core_block, basis_y, precision=HIGH)
    columns = basis_x
    decoded = jnp.einsum(
        "xa,ayk->xyk", columns, lax.all_gather(mixed_y, "gx", axis=0, tiled=True), precision=HIGH
    )
    decoded = decoded.reshape(rows_x, rows_y, rank_z, rank_v)
    back_v = jnp.einsum("xyrs,vs->vxyr", decoded, basis_v, precision=HIGH)
    recon = jnp.einsum("vxyr,zr->vxyz", back_v, basis_z, precision=HIGH)
    error = state - recon
    miss_local = jnp.sum(error * error, axis=(1, 2, 3))
    mass_local = jnp.sum(state * state, axis=(1, 2, 3))
    miss, mass = lax.psum((miss_local, mass_local), ("gx", "gy"))
    residual = jnp.sqrt(miss / (mass + 1e-06))
    return (state, recon, residual)


def solution(mesh):
    return jax.shard_map(
        on_device,
        mesh=mesh,
        in_specs=(
            P(None, "gx", "gy", None),
            P(),
            P(),
            P(),
            P(),
            P("gx", None),
            P("gy", None),
            P(),
            P(),
        ),
        out_specs=(P(None, "gx", "gy", None), P(None, "gx", "gy", None), P()),
        check_vma=False,
    )
```

profile of v0, /device:TPU:0, one launch (start us, length us, event | category | flops | bytes accessed | tf_op | source)
XLA Modules:
  0.0 209.1 jit_solution(7740615977400366910)
XLA Ops:
  7.2 1.0 fusion.57
  8.3 2.4 %collective-permute-start = (f32[12,2,8,128]{3,0,2,1:T(8,128)S(1)}, f32[12,2,8,128]{3,0,2,1:T(8,128)S(1)}, u32[]{:S(2)}, u32[]{:S(2)}) collective-permute-start(f32[12,2,8,128]{3,0,2,1:T(8,128)S(1)} %copy.76), channel_id=1, source_target_pairs={{0,8},{8,16},{16,24},{1,9},{9,17},{17,25},{2,10},{10,18},{18,26},{... | collective-permute-start | bytes 294920 | tf_op jit(solution)/shard_map/ppermute | solution.py:16
  10.8 1.3 collective-permute-start.1
  12.1 0.5 copy_dynamic-update-slice_fusion
  12.6 3.5 %collective-permute-done.1 = f32[12,2,8,128]{3,0,2,1:T(8,128)S(1)} collective-permute-done((f32[12,2,8,128]{3,0,2,1:T(8,128)S(1)}, f32[12,2,8,128]{3,0,2,1:T(8,128)S(1)}, u32[]{:S(2)}, u32[]{:S(2)}) %collective-permute-start.1) | collective-permute-done | bytes 98336 | tf_op jit(solution)/shard_map/ppermute | solution.py:17
  16.2 3.4 %collective-permute-start.2 = (f32[12,20,2,128]{3,0,2,1:T(8,128)S(1)}, f32[12,20,2,128]{3,0,2,1:T(8,128)S(1)}, u32[]{:S(2)}, u32[]{:S(2)}) collective-permute-start(f32[12,20,2,128]{3,0,2,1:T(8,128)S(1)} %get-tuple-element.19), channel_id=1, source_target_pairs={{0,1},{1,2},{2,3},{3,4},{4,5},{5,6},{6,7},{8,9},{9,10},{10,11},{11... | collective-permute-start | bytes 737288 | tf_op jit(solution)/shard_map/ppermute | solution.py:16
  19.6 1.3 collective-permute-start.3
  21.0 4.2 %collective-permute-done.2 = f32[12,20,2,128]{3,0,2,1:T(8,128)S(1)} collective-permute-done((f32[12,20,2,128]{3,0,2,1:T(8,128)S(1)}, f32[12,20,2,128]{3,0,2,1:T(8,128)S(1)}, u32[]{:S(2)}, u32[]{:S(2)}) %collective-permute-start.2) | collective-permute-done | bytes 245792 | tf_op jit(solution)/shard_map/ppermute | solution.py:16
  25.2 4.6 %collective-permute-done.3 = f32[12,20,2,128]{3,0,2,1:T(8,128)S(1)} collective-permute-done((f32[12,20,2,128]{3,0,2,1:T(8,128)S(1)}, f32[12,20,2,128]{3,0,2,1:T(8,128)S(1)}, u32[]{:S(2)}, u32[]{:S(2)}) %collective-permute-start.3) | collective-permute-done | bytes 245792 | tf_op jit(solution)/shard_map/ppermute | solution.py:17
  29.8 0.2 pad_maximum_fusion
  30.0 0.1 fusion.41
  30.1 2.3 %fusion.8 = f32[12,18,10,128]{3,0,2,1:T(8,128)S(1)} fusion(f32[12,20,12,128]{3,0,2,1:T(8,128)S(1)} %pad_maximum_fusion, f32[12,20,8,128]{3,0,2,1:T(8,128)S(1)} %constant_dynamic-update-slice_fusion, f32[12,20,2,128]{3,0,2,1:T(8,128)S(1)} %collective-permute-done.2, f32[12,20,2,128]{3,0,2,1:T(8,128)S(1)} %collective-permute-done.3, ...), kind=kOutput, calls=%fused_computation.14 | convolution fusion | flops 44236800 | bytes 11096576 | tf_op jit(solution)/shard_map/vw,wxyz->vxyz/dot_general | solution.py:38
  32.6 2.2 %fusion.23 = f32[12,16,8,128]{3,0,2,1:T(8,128)S(1)} fusion(f32[12,18,10,128]{3,0,2,1:T(8,128)S(1)} %fusion.8, f32[16,8,128]{2,1,0:T(8,128)S(1)} %bitcast.62, f32[12]{0:T(128)S(1)} %neg.5, f32[12]{0:T(128)S(1)} %copy-done.8, f32[12]{0:T(128)S(1)} %copy-done.9, f32[12,16,8,128]{3,2,1,0:T(8,128)S(1)} %copy-done.2, f32[12,12]{1,0:T(8,128)S(1)} %copy-done.6), kind=kOutput, calls=%fused_computation.37 | convolution fusion | flops 31260672 | bytes 9414144 | tf_op jit(solution)/shard_map/vw,wxyz->vxyz/dot_general | solution.py:38
  34.8 1.0 fusion.44
  35.8 0.7 fusion.51
  36.5 0.5 copy.49
  37.1 1.7 convolution_bitcast_fusion.3
  38.7 1.1 copy.51
  39.9 27.8 %reduce-scatter.2.cloned.1.call-done = f32[16,8,192]{2,1,0:T(8,128)} async-done(((f32[64,8,192]{2,1,0:T(8,128)}), f32[16,8,192]{2,1,0:T(8,128)}) %reduce-scatter.2.cloned.1.call-update) | async-done | bytes 98320 | tf_op jit(solution)/shard_map/reduce_scatter | solution.py:77
  67.7 2.9 %convolution_bitcast_fusion.1 = f32[16,64,192]{2,1,0:T(8,128)} fusion(f32[16,8,192]{2,1,0:T(8,128)} %reduce-scatter.2.cloned.1.call-done, f32[8,64]{1,0:T(8,128)S(1)} %copy-done.4), kind=kOutput, calls=%fused_computation.23 | convolution fusion | flops 18874368 | bytes 886784 | tf_op jit(solution)/shard_map/ayk,yb->abk/dot_general | solution.py:83
  70.6 1.1 copy.57
  71.7 77.8 %all-reduce.5.cloned.1.call-done = f32[16,64,192]{2,1,0:T(8,128)} async-done(((f32[16,64,192]{2,1,0:T(8,128)}), f32[16,64,192]{2,1,0:T(8,128)}) %all-reduce.5.cloned.1.call-update) | async-done | bytes 786448 | tf_op jit(solution)/shard_map/psum | solution.py:84
  149.5 1.9 convolution_bitcast_fusion.5
  151.3 7.3 %all_gather.3 = f32[64,8,192]{2,1,0:T(8,128)S(1)} all-gather(f32[16,8,192]{2,1,0:T(8,128)S(1)} %convolution_bitcast_fusion.5), channel_id=1, replica_groups=mesh['gx'=4,'gy'=8] {'gx'}, dimensions={0}, use_global_device_ids=true | all-gather | bytes 491520 | tf_op jit(solution)/shard_map/all_gather | solution.py:88
  158.7 0.5 convolution_bitcast_fusion.4
  159.2 0.3 copy.53
  159.5 0.6 copy.54
  160.1 1.0 convolution_bitcast_fusion
  161.2 0.9 fusion.31
  162.1 0.7 multiply_reduce_fusion
  162.8 38.9 %all-reduce.2 = (f32[12]{0:T(128)S(1)}, f32[12]{0:T(128)S(1)}) all-reduce(f32[12]{0:T(128)S(1)} %get-tuple-element.16, f32[12]{0:T(128)S(1)} %get-tuple-element.15), channel_id=1, replica_groups=mesh['gx'=4,'gy'=8] {'gx','gy'}, use_global_device_ids=true, to_apply=%region_3.4 | all-reduce | flops 24 | bytes 192 | tf_op jit(solution)/shard_map/psum | solution.py:96
  201.7 0.5 fusion.55
  (36 shorter events, 0.5 us)
Async XLA Ops:
  7.2 27.6 %copy-start = (f32[128,32]{0,1:T(8,128)S(1)}, f32[128,32]{0,1:T(8,128)}, u32[]{:S(2)}) copy-start(f32[128,32]{0,1:T(8,128)} %param.16) | copy-start | bytes 49156
  7.2 4.9 %copy-start.2 = (f32[12,16,8,128]{3,2,1,0:T(8,128)S(1)}, f32[12,16,8,128]{3,2,1,0:T(8,128)}, u32[]{:S(2)}) copy-start(f32[12,16,8,128]{3,2,1,0:T(8,128)} %param.9) | copy-start | bytes 2359300
  7.2 60.5 %reduce-scatter.2.cloned.1.call-start = ((), (), s32[]{:S(2)}) async-start(), calls=%async_computation.1 | async-start | bytes 655360 | tf_op jit(solution)/shard_map/reduce_scatter | solution.py:77
  8.3 3.8 %collective-permute-start = (f32[12,2,8,128]{3,0,2,1:T(8,128)S(1)}, f32[12,2,8,128]{3,0,2,1:T(8,128)S(1)}, u32[]{:S(2)}, u32[]{:S(2)}) collective-permute-start(f32[12,2,8,128]{3,0,2,1:T(8,128)S(1)} %copy.76), channel_id=1, source_target_pairs={{0,8},{8,16},{16,24},{1,9},{9,17},{17,25},{2,10},{10,18},{18,26},{... | collective-permute-start | bytes 294920 | tf_op jit(solution)/shard_map/ppermute | solution.py:16
  10.8 5.3 %collective-permute-start.1 = (f32[12,2,8,128]{3,0,2,1:T(8,128)S(1)}, f32[12,2,8,128]{3,0,2,1:T(8,128)S(1)}, u32[]{:S(2)}, u32[]{:S(2)}) collective-permute-start(f32[12,2,8,128]{3,0,2,1:T(8,128)S(1)} %copy.77), channel_id=1, source_target_pairs={{8,0},{16,8},{24,16},{9,1},{17,9},{25,17},{10,2},{18,10},{26,18},{... | collective-permute-start | bytes 294920 | tf_op jit(solution)/shard_map/ppermute | solution.py:17
  12.1 8.8 %copy-start.7 = (f32[12]{0:T(128)S(1)}, f32[12]{0:T(128)}, u32[]{:S(2)}) copy-start(f32[12]{0:T(128)} %param.12) | copy-start | bytes 148
  16.2 9.0 %collective-permute-start.2 = (f32[12,20,2,128]{3,0,2,1:T(8,128)S(1)}, f32[12,20,2,128]{3,0,2,1:T(8,128)S(1)}, u32[]{:S(2)}, u32[]{:S(2)}) collective-permute-start(f32[12,20,2,128]{3,0,2,1:T(8,128)S(1)} %get-tuple-element.19), channel_id=1, source_target_pairs={{0,1},{1,2},{2,3},{3,4},{4,5},{5,6},{6,7},{8,9},{9,10},{10,11},{11... | collective-permute-start | bytes 737288 | tf_op jit(solution)/shard_map/ppermute | solution.py:16
  19.6 10.2 %collective-permute-start.3 = (f32[12,20,2,128]{3,0,2,1:T(8,128)S(1)}, f32[12,20,2,128]{3,0,2,1:T(8,128)S(1)}, u32[]{:S(2)}, u32[]{:S(2)}) collective-permute-start(f32[12,20,2,128]{3,0,2,1:T(8,128)S(1)} %get-tuple-element.20), channel_id=1, source_target_pairs={{1,0},{2,1},{3,2},{4,3},{5,4},{6,5},{7,6},{9,8},{10,9},{11,10},{12... | collective-permute-start | bytes 737288 | tf_op jit(solution)/shard_map/ppermute | solution.py:17
  21.0 9.1 %copy-start.6 = (f32[12,12]{1,0:T(8,128)S(1)}, f32[12,12]{1,0:T(8,128)}, u32[]{:S(2)}) copy-start(f32[12,12]{1,0:T(8,128)} %param.13) | copy-start | bytes 1732
  21.0 9.1 %copy-start.8 = (f32[12]{0:T(128)S(1)}, f32[12]{0:T(128)}, u32[]{:S(2)}) copy-start(f32[12]{0:T(128)} %param.11) | copy-start | bytes 148
  21.0 9.1 %copy-start.9 = (f32[12]{0:T(128)S(1)}, f32[12]{0:T(128)}, u32[]{:S(2)}) copy-start(f32[12]{0:T(128)} %param.10) | copy-start | bytes 148
  34.8 1.0 copy-start.5
  35.8 1.3 copy-start.3
  37.1 30.6 %copy-start.4 = (f32[8,64]{1,0:T(8,128)S(1)}, f32[8,64]{1,0:T(8,128)}, u32[]{:S(2)}) copy-start(f32[8,64]{1,0:T(8,128)} %param.15) | copy-start | bytes 6148
  39.9 109.6 %all-reduce.5.cloned.1.call-start = ((), (), s32[]{:S(2)}) async-start(), calls=%async_computation.2 | async-start | bytes 2097152 | tf_op jit(solution)/shard_map/psum | solution.py:84
  162.1 40.1 %copy-start.1 = (f32[12,16,8,128]{3,2,1,0:T(8,128)}, f32[12,16,8,128]{3,2,1,0:T(8,128)S(1)}, u32[]{:S(2)}) copy-start(f32[12,16,8,128]{3,2,1,0:T(8,128)S(1)} %fusion.31) | copy-start | bytes 2359300
Sparse Core Ops, SparseCore 0:
  40.0 27.6 reduce-scatter.1
  71.2 78.2 all-reduce.4
where the time goes:
time: 209 us
  waiting for transfers between devices  118 us (56%)
  blocking collectives  46.3 us (22%)
  matrix products  15.1 us (7%)
  between operations  14.4 us (7%)
  starting transfers between devices  8.51 us (4%)
  local copies, waits for them, and re-layouts  5.35 us (3%)
    psum x1, waiting for transfers between devices, on_device(): core_block = lax.psum(core_block, 'gy')  77.8 us
    psum x1, blocking collectives, on_device(): miss, mass = lax.psum((miss_local, mass_local), ('gx', 'gy'))  38.9 us
    reduce_scatter x1, waiting for transfers between devices, on_device(): lax.psum_scatter(jnp.einsum('xa,xyk->ayk', columns, packed, precision=HIG...  27.8 us
    ppermute x2, waiting for transfers between devices, padded_2(): after = lax.ppermute(first, axis, down)  8.07 us
    all_gather x1, blocking collectives, on_device(): lax.all_gather(mixed_y, 'gx', axis=0, tiled=True)  7.32 us
    ppermute x2, starting transfers between devices, padded_2(): before = lax.ppermute(last, axis, up)  5.85 us
    dot_general x2, matrix products, reaction(): return jnp.einsum('vw,wxyz->vxyz', mixing, rate_terms, precision=HIGH)  4.55 us
  transfers between devices with their start and end apart: 6, of which 5 were waited for; matrix products, arithmetic and copies ran while one was open for 1% of the time, Pallas kernels for 0%

commit v1 on v0

--- a/solution.py
+++ b/solution.py
@@ -81,7 +81,11 @@
         tiled=True,
     )
     core_block = jnp.einsum("ayk,yb->abk", part_x, basis_y, precision=HIGH)
-    core_block = lax.psum(core_block, "gy")
+    peers_2, acc = (lax.axis_size("gy"), core_block)
+    for far in [1 << k for k in range(peers_2.bit_length() - 1)]:
+        swap = [(i_2, i_2 ^ far) for i_2 in range(peers_2)]
+        acc = acc + lax.ppermute(acc, "gy", swap)
+    core_block = acc
     mixed_y = jnp.einsum("abk,yb->ayk", core_block, basis_y, precision=HIGH)
     columns = basis_x
     decoded = jnp.einsum(

time: 209 us -> 223 us (1.067)
  waiting for transfers between devices: 118 us -> 129 us
  starting transfers between devices: 8.51 us -> 14.1 us
  matrix products: 15.1 us -> 12.8 us
    ppermute x0 -> x3, waiting for transfers between devices: none -> 88.5 us  [on_device(): acc = acc + lax.ppermute(acc, 'gy', swap)]
    psum x1 -> x0, waiting for transfers between devices: 77.8 us -> none  [on_device(): core_block = lax.psum(core_block, 'gy')]
    ppermute x0 -> x3, starting transfers between devices: none -> 5.6 us  [on_device(): acc = acc + lax.ppermute(acc, 'gy', swap)]
  transfers between devices with their start and end apart: 6 -> 8, of which waited for: 5 -> 7; matrix products, arithmetic and copies ran while one was open for 1% -> 1% of each run, Pallas kernels for 0% -> 0%
where the time goes in v1:
time: 223 us
  waiting for transfers between devices  129 us (58%)
  blocking collectives  45.9 us (21%)
  between operations  14.4 us (6%)
  starting transfers between devices  14.1 us (6%)
  matrix products  12.8 us (6%)
  local copies, waits for them, and re-layouts  5.4 us (2%)
    ppermute x3, waiting for transfers between devices, on_device(): acc = acc + lax.ppermute(acc, 'gy', swap)  88.5 us
    psum x1, blocking collectives, on_device(): miss, mass = lax.psum((miss_local, mass_local), ('gx', 'gy'))  39.1 us
    reduce_scatter x1, waiting for transfers between devices, on_device(): lax.psum_scatter(jnp.einsum('xa,xyk->ayk', columns, packed, precision=HIG...  27.8 us
    ppermute x2, waiting for transfers between devices, padded_2(): after = lax.ppermute(first, axis, down)  8.07 us
    all_gather x1, blocking collectives, on_device(): lax.all_gather(mixed_y, 'gx', axis=0, tiled=True)  6.78 us
    ppermute x2, starting transfers between devices, padded_2(): before = lax.ppermute(last, axis, up)  5.85 us
    ppermute x3, starting transfers between devices, on_device(): acc = acc + lax.ppermute(acc, 'gy', swap)  5.6 us
    dot_general x2, matrix products, reaction(): return jnp.einsum('vw,wxyz->vxyz', mixing, rate_terms, precision=HIGH)  4.55 us
  transfers between devices with their start and end apart: 8, of which 7 were waited for; matrix products, arithmetic and copies ran while one was open for 1% of the time, Pallas kernels for 0%

profile of v1, /device:TPU:0, one launch (start us, length us, event | category | flops | bytes accessed | tf_op | source)
XLA Modules:
  0.0 223.1 jit_solution(2104366885545758304)
XLA Ops:
  7.2 1.0 fusion.61
  8.3 2.4 %collective-permute-start = (f32[12,2,8,128]{3,0,2,1:T(8,128)S(1)}, f32[12,2,8,128]{3,0,2,1:T(8,128)S(1)}, u32[]{:S(2)}, u32[]{:S(2)}) collective-permute-start(f32[12,2,8,128]{3,0,2,1:T(8,128)S(1)} %copy.53), channel_id=1, source_target_pairs={{0,8},{8,16},{16,24},{1,9},{9,17},{17,25},{2,10},{10,18},{18,26},{... | collective-permute-start | bytes 294920 | tf_op jit(solution)/shard_map/ppermute | solution.py:16
  10.8 1.3 collective-permute-start.1
  12.6 3.5 %collective-permute-done.1 = f32[12,2,8,128]{3,0,2,1:T(8,128)S(1)} collective-permute-done((f32[12,2,8,128]{3,0,2,1:T(8,128)S(1)}, f32[12,2,8,128]{3,0,2,1:T(8,128)S(1)}, u32[]{:S(2)}, u32[]{:S(2)}) %collective-permute-start.1) | collective-permute-done | bytes 98336 | tf_op jit(solution)/shard_map/ppermute | solution.py:17
  16.2 3.4 %collective-permute-start.2 = (f32[12,20,2,128]{3,0,2,1:T(8,128)S(1)}, f32[12,20,2,128]{3,0,2,1:T(8,128)S(1)}, u32[]{:S(2)}, u32[]{:S(2)}) collective-permute-start(f32[12,20,2,128]{3,0,2,1:T(8,128)S(1)} %get-tuple-element.13), channel_id=1, source_target_pairs={{0,1},{1,2},{2,3},{3,4},{4,5},{5,6},{6,7},{8,9},{9,10},{10,11},{11... | collective-permute-start | bytes 737288 | tf_op jit(solution)/shard_map/ppermute | solution.py:16
  19.6 1.3 collective-permute-start.3
  21.0 4.2 %collective-permute-done.2 = f32[12,20,2,128]{3,0,2,1:T(8,128)S(1)} collective-permute-done((f32[12,20,2,128]{3,0,2,1:T(8,128)S(1)}, f32[12,20,2,128]{3,0,2,1:T(8,128)S(1)}, u32[]{:S(2)}, u32[]{:S(2)}) %collective-permute-start.2) | collective-permute-done | bytes 245792 | tf_op jit(solution)/shard_map/ppermute | solution.py:16
  25.2 4.6 %collective-permute-done.3 = f32[12,20,2,128]{3,0,2,1:T(8,128)S(1)} collective-permute-done((f32[12,20,2,128]{3,0,2,1:T(8,128)S(1)}, f32[12,20,2,128]{3,0,2,1:T(8,128)S(1)}, u32[]{:S(2)}, u32[]{:S(2)}) %collective-permute-start.3) | collective-permute-done | bytes 245792 | tf_op jit(solution)/shard_map/ppermute | solution.py:17
  30.1 2.3 %fusion.8 = f32[12,18,10,128]{3,0,2,1:T(8,128)S(1)} fusion(f32[12,20,12,128]{3,0,2,1:T(8,128)S(1)} %pad_maximum_fusion, f32[12,20,8,128]{3,0,2,1:T(8,128)S(1)} %constant_dynamic-update-slice_fusion, f32[12,20,2,128]{3,0,2,1:T(8,128)S(1)} %collective-permute-done.2, f32[12,20,2,128]{3,0,2,1:T(8,128)S(1)} %collective-permute-done.3, ...), kind=kOutput, calls=%fused_computation.14 | convolution fusion | flops 44236800 | bytes 11096576 | tf_op jit(solution)/shard_map/vw,wxyz->vxyz/dot_general | solution.py:38
  32.6 2.2 fusion.23
  34.8 1.0 fusion.47
  35.8 0.7 fusion.55
  36.5 0.5 copy.24
  37.1 1.7 fusion.36
  38.7 1.1 copy.55
  39.9 27.8 %reduce-scatter.2.cloned.1.call-done = f32[16,8,192]{2,1,0:T(8,128)} async-done(((f32[64,8,192]{2,1,0:T(8,128)}), f32[16,8,192]{2,1,0:T(8,128)}) %reduce-scatter.2.cloned.1.call-update) | async-done | bytes 98320 | tf_op jit(solution)/shard_map/reduce_scatter | solution.py:77
  67.7 1.9 convolution_bitcast_fusion
  69.6 1.6 collective-permute-start.4
  71.2 23.2 %collective-permute-done.4 = f32[16,64,192]{2,1,0:T(8,128)S(1)} collective-permute-done((f32[16,64,192]{2,1,0:T(8,128)S(1)}, f32[16,64,192]{2,1,0:T(8,128)S(1)}, u32[]{:S(2)}, u32[]{:S(2)}) %collective-permute-start.4) | collective-permute-done | bytes 786464 | tf_op jit(solution)/shard_map/ppermute | solution.py:87
  94.6 1.6 collective-permute-start.5
  96.1 22.4 %collective-permute-done.5 = f32[16,64,192]{2,1,0:T(8,128)S(1)} collective-permute-done((f32[16,64,192]{2,1,0:T(8,128)S(1)}, f32[16,64,192]{2,1,0:T(8,128)S(1)}, u32[]{:S(2)}, u32[]{:S(2)}) %collective-permute-start.5) | collective-permute-done | bytes 786464 | tf_op jit(solution)/shard_map/ppermute | solution.py:87
  118.7 2.5 %collective-permute-start.6 = (f32[16,64,192]{2,1,0:T(8,128)S(1)}, f32[16,64,192]{2,1,0:T(8,128)S(1)}, u32[]{:S(2)}, u32[]{:S(2)}) collective-permute-start(f32[16,64,192]{2,1,0:T(8,128)S(1)} %add.135), channel_id=1, source_target_pairs={{0,4},{1,5},{2,6},{3,7},{4,0},{5,1},{6,2},{7,3},{8,12},{9,13},{10,... | collective-permute-start | bytes 2359304 | tf_op jit(solution)/shard_map/ppermute | solution.py:87
  121.2 1.1 copy.27
  122.3 42.9 %collective-permute-done.6 = f32[16,64,192]{2,1,0:T(8,128)S(1)} collective-permute-done((f32[16,64,192]{2,1,0:T(8,128)S(1)}, f32[16,64,192]{2,1,0:T(8,128)S(1)}, u32[]{:S(2)}, u32[]{:S(2)}) %collective-permute-start.6) | collective-permute-done | bytes 786464 | tf_op jit(solution)/shard_map/ppermute | solution.py:87
  165.1 0.7 fusion.26
  165.9 6.8 %all_gather.3 = f32[64,8,192]{2,0,1:T(8,128)S(1)} all-gather(f32[16,8,192]{2,0,1:T(8,128)S(1)} %bitcast.65), channel_id=1, replica_groups=mesh['gx'=4,'gy'=8] {'gx'}, dimensions={0}, use_global_device_ids=true | all-gather | bytes 491520 | tf_op jit(solution)/shard_map/all_gather | solution.py:92
  173.4 0.6 copy.34
  174.0 1.0 fusion.53
  175.0 0.9 fusion.33
  176.0 0.7 multiply_reduce_fusion
  176.6 39.1 %all-reduce.2 = (f32[12]{0:T(128)S(1)}, f32[12]{0:T(128)S(1)}) all-reduce(f32[12]{0:T(128)S(1)} %get-tuple-element.10, f32[12]{0:T(128)S(1)} %get-tuple-element.9), channel_id=1, replica_groups=mesh['gx'=4,'gy'=8] {'gx','gy'}, use_global_device_ids=true, to_apply=%region_2.3 | all-reduce | flops 24 | bytes 192 | tf_op jit(solution)/shard_map/psum | solution.py:100
  215.8 0.5 fusion.59
  (42 shorter events, 2.3 us)
Async XLA Ops:
  7.2 27.6 %copy-start = (f32[128,32]{0,1:T(8,128)S(1)}, f32[128,32]{0,1:T(8,128)}, u32[]{:S(2)}) copy-start(f32[128,32]{0,1:T(8,128)} %param.16) | copy-start | bytes 49156
  7.2 4.9 %copy-start.2 = (f32[12,16,8,128]{3,2,1,0:T(8,128)S(1)}, f32[12,16,8,128]{3,2,1,0:T(8,128)}, u32[]{:S(2)}) copy-start(f32[12,16,8,128]{3,2,1,0:T(8,128)} %param.9) | copy-start | bytes 2359300
  7.2 60.5 %reduce-scatter.2.cloned.1.call-start = ((), (), s32[]{:S(2)}) async-start(), calls=%async_computation.1 | async-start | bytes 655360 | tf_op jit(solution)/shard_map/reduce_scatter | solution.py:77
  8.3 3.8 %collective-permute-start = (f32[12,2,8,128]{3,0,2,1:T(8,128)S(1)}, f32[12,2,8,128]{3,0,2,1:T(8,128)S(1)}, u32[]{:S(2)}, u32[]{:S(2)}) collective-permute-start(f32[12,2,8,128]{3,0,2,1:T(8,128)S(1)} %copy.53), channel_id=1, source_target_pairs={{0,8},{8,16},{16,24},{1,9},{9,17},{17,25},{2,10},{10,18},{18,26},{... | collective-permute-start | bytes 294920 | tf_op jit(solution)/shard_map/ppermute | solution.py:16
  10.8 5.3 %collective-permute-start.1 = (f32[12,2,8,128]{3,0,2,1:T(8,128)S(1)}, f32[12,2,8,128]{3,0,2,1:T(8,128)S(1)}, u32[]{:S(2)}, u32[]{:S(2)}) collective-permute-start(f32[12,2,8,128]{3,0,2,1:T(8,128)S(1)} %copy.54), channel_id=1, source_target_pairs={{8,0},{16,8},{24,16},{9,1},{17,9},{25,17},{10,2},{18,10},{26,18},{... | collective-permute-start | bytes 294920 | tf_op jit(solution)/shard_map/ppermute | solution.py:17
  12.1 8.8 %copy-start.7 = (f32[12]{0:T(128)S(1)}, f32[12]{0:T(128)}, u32[]{:S(2)}) copy-start(f32[12]{0:T(128)} %param.12) | copy-start | bytes 148
  16.2 9.0 %collective-permute-start.2 = (f32[12,20,2,128]{3,0,2,1:T(8,128)S(1)}, f32[12,20,2,128]{3,0,2,1:T(8,128)S(1)}, u32[]{:S(2)}, u32[]{:S(2)}) collective-permute-start(f32[12,20,2,128]{3,0,2,1:T(8,128)S(1)} %get-tuple-element.13), channel_id=1, source_target_pairs={{0,1},{1,2},{2,3},{3,4},{4,5},{5,6},{6,7},{8,9},{9,10},{10,11},{11... | collective-permute-start | bytes 737288 | tf_op jit(solution)/shard_map/ppermute | solution.py:16
  19.6 10.2 %collective-permute-start.3 = (f32[12,20,2,128]{3,0,2,1:T(8,128)S(1)}, f32[12,20,2,128]{3,0,2,1:T(8,128)S(1)}, u32[]{:S(2)}, u32[]{:S(2)}) collective-permute-start(f32[12,20,2,128]{3,0,2,1:T(8,128)S(1)} %get-tuple-element.14), channel_id=1, source_target_pairs={{1,0},{2,1},{3,2},{4,3},{5,4},{6,5},{7,6},{9,8},{10,9},{11,10},{12... | collective-permute-start | bytes 737288 | tf_op jit(solution)/shard_map/ppermute | solution.py:17
  21.0 9.1 %copy-start.6 = (f32[12,12]{1,0:T(8,128)S(1)}, f32[12,12]{1,0:T(8,128)}, u32[]{:S(2)}) copy-start(f32[12,12]{1,0:T(8,128)} %param.13) | copy-start | bytes 1732
  21.0 9.1 %copy-start.8 = (f32[12]{0:T(128)S(1)}, f32[12]{0:T(128)}, u32[]{:S(2)}) copy-start(f32[12]{0:T(128)} %param.11) | copy-start | bytes 148
  21.0 9.1 %copy-start.9 = (f32[12]{0:T(128)S(1)}, f32[12]{0:T(128)}, u32[]{:S(2)}) copy-start(f32[12]{0:T(128)} %param.10) | copy-start | bytes 148
  34.8 1.0 copy-start.5
  35.8 1.3 copy-start.3
  37.1 30.6 %copy-start.4 = (f32[8,64]{1,0:T(8,128)S(1)}, f32[8,64]{1,0:T(8,128)}, u32[]{:S(2)}) copy-start(f32[8,64]{1,0:T(8,128)} %param.15) | copy-start | bytes 6148
  69.6 24.8 %collective-permute-start.4 = (f32[16,64,192]{2,1,0:T(8,128)S(1)}, f32[16,64,192]{2,1,0:T(8,128)S(1)}, u32[]{:S(2)}, u32[]{:S(2)}) collective-permute-start(f32[16,64,192]{2,1,0:T(8,128)S(1)} %convolution_bitcast_fusion), channel_id=1, source_target_pairs={{0,1},{1,0},{2,3},{3,2},{4,5},{5,4},{6,7},{7,6},{8,9},{9,8},{10,11... | collective-permute-start | bytes 2359304 | tf_op jit(solution)/shard_map/ppermute | solution.py:87
  94.6 23.9 %collective-permute-start.5 = (f32[16,64,192]{2,1,0:T(8,128)S(1)}, f32[16,64,192]{2,1,0:T(8,128)S(1)}, u32[]{:S(2)}, u32[]{:S(2)}) collective-permute-start(f32[16,64,192]{2,1,0:T(8,128)S(1)} %add.134), channel_id=1, source_target_pairs={{0,2},{1,3},{2,0},{3,1},{4,6},{5,7},{6,4},{7,5},{8,10},{9,11},{10,... | collective-permute-start | bytes 2359304 | tf_op jit(solution)/shard_map/ppermute | solution.py:87
  118.7 46.5 %collective-permute-start.6 = (f32[16,64,192]{2,1,0:T(8,128)S(1)}, f32[16,64,192]{2,1,0:T(8,128)S(1)}, u32[]{:S(2)}, u32[]{:S(2)}) collective-permute-start(f32[16,64,192]{2,1,0:T(8,128)S(1)} %add.135), channel_id=1, source_target_pairs={{0,4},{1,5},{2,6},{3,7},{4,0},{5,1},{6,2},{7,3},{8,12},{9,13},{10,... | collective-permute-start | bytes 2359304 | tf_op jit(solution)/shard_map/ppermute | solution.py:87
  176.0 40.3 %copy-start.1 = (f32[12,16,8,128]{3,2,1,0:T(8,128)}, f32[12,16,8,128]{3,2,1,0:T(8,128)S(1)}, u32[]{:S(2)}) copy-start(f32[12,16,8,128]{3,2,1,0:T(8,128)S(1)} %fusion.33) | copy-start | bytes 2359300
Sparse Core Ops, SparseCore 0:
  40.0 27.6 reduce-scatter.1
